TPU v7x, 256 devices: a whole 4x4x8 slice. The times are simulated.
256 devices in a mesh: row: 16 (over x, z_hi, core), col: 16 (over z_lo, y).
Axes of the slice: x: 4, y: 4, z: 8 (z_hi: 2, z_lo: 4; z = z_hi * 4 + z_lo), core: 2. Of those that a mesh axis runs over, the one named last changes fastest.
Arguments:
- diag_coords: int32 [2, 1536], replicated, may hold values from 0 to 32767
- panel_coords: int32 [2, 16, 1536], P(None, 'row', 'col'), may hold values from 0 to 32767
- test_matrix: bfloat16 [16, 1536, 512], P('row', 'col'), may hold values from -6 to 6
- ranks: int32 [16], replicated, may hold values from 64 to 512, as said below
Outputs:
- panel_left: bfloat16 [16, 1536, 512], P('row', 'col')
- update_right: bfloat16 [16, 16, 1536, 512], P('row', 'col')
Inputs may be any that keep to these rules, and one draw needn't show every extreme that they name: ranks[i] is 512 at tile 0 and 64 at the last tile and falls roughly evenly in between, with small random steps.
All inputs are finite; a program needn't handle non-finite values.
Results may differ from a plain program's by a relative error of at most 0.0068.
Values may be sent and summed in bfloat16 or wider, within the bound.
No kernel may reach another device: no remote copies, remote signals or barrier semaphores. Data moves between devices by JAX's collectives and lax.ppermute only.
A program may use at most 192 MiB of HBM per device.

v0:
```python
import jax
import jax.numpy as jnp
from jax import lax
from jax.sharding import PartitionSpec as P

range_length = 409.6
nugget = 0.5
shift_ratio = 0.01


def broadcast(value, axis, root):
    mine = lax.axis_index(axis) == root
    return lax.psum(jnp.where(mine, value, jnp.zeros_like(value)), axis)


def matern(first, second):
    delta_x = (first[0][:, None] - second[0][None, :]).astype(jnp.float32)
    delta_y = (first[1][:, None] - second[1][None, :]).astype(jnp.float32)
    return jnp.exp(-jnp.sqrt(delta_x * delta_x + delta_y * delta_y) / range_length)


def solve_right(factor, sample):
    return jax.scipy.linalg.solve_triangular(factor, sample.T, lower=True).T


def shards(diag_coords, panel_coords, test_matrix, ranks):
    points = diag_coords.shape[1]
    row_tiles = panel_coords.shape[1]
    width = test_matrix.shape[2]
    n_row = lax.axis_size("row")
    n_col = lax.axis_size("col")
    col_tiles = row_tiles * n_row // n_col
    row_index = lax.axis_index("row")
    col_index = lax.axis_index("col")
    cov = matern(diag_coords, diag_coords) + nugget * jnp.eye(points, dtype=jnp.float32)
    is_owner = (row_index == 0) & (col_index == 0)
    lower = lax.cond(is_owner, jnp.linalg.cholesky, jnp.zeros_like, cov)
    lower = broadcast(lower, ("row", "col"), 0)
    columns = jnp.arange(width, dtype=jnp.int32)
    row_ranks = lax.dynamic_slice_in_dim(ranks, row_index * row_tiles, row_tiles)
    row_mask = (columns[None, :] < row_ranks[:, None]).astype(jnp.float32)
    tests_full = lax.all_gather(test_matrix, "col", axis=1, tiled=True)
    tests_rows = tests_full * row_mask.astype(jnp.bfloat16)[:, None, :]
    local_points = panel_coords.reshape(2, -1)
    block = matern(local_points, diag_coords)
    solved = jax.scipy.linalg.solve_triangular(lower, block.T, lower=True).T
    solved = solved.reshape(row_tiles, -1, points)
    sample = jnp.einsum(
        "inm,imr->inr", solved, tests_rows.astype(jnp.float32), precision=lax.Precision.HIGHEST
    )
    gram_part = jnp.einsum("inr,ins->irs", sample, sample, precision=lax.Precision.HIGHEST)
    gram = lax.psum(gram_part, "col")
    trace = jnp.sum(jnp.diagonal(gram, axis1=1, axis2=2), axis=1)
    shift = shift_ratio * trace / row_ranks.astype(jnp.float32)
    extra = shift[:, None] * row_mask + 1.0 - row_mask
    shifted = gram + extra[:, :, None] * jnp.eye(width, dtype=jnp.float32)[None]
    factor = jnp.linalg.cholesky(shifted)
    left = jax.vmap(solve_right)(factor, sample).astype(jnp.bfloat16)
    coeff_part = jnp.einsum(
        "inm,inr->imr", solved, left.astype(jnp.float32), precision=lax.Precision.HIGHEST
    )
    coeff_piece = lax.psum_scatter(coeff_part, "col", scatter_dimension=1, tiled=True).astype(
        jnp.bfloat16
    )
    coeff = lax.all_gather(coeff_piece, "col", axis=1, tiled=True)
    left_full = lax.all_gather(left, "col", axis=1, tiled=True)
    root = col_index * col_tiles // row_tiles
    stacked = jnp.stack([left_full, coeff])
    slab = broadcast(stacked, "row", root)
    offset = col_index * col_tiles % row_tiles
    col_left = slab[0]
    col_coeff = slab[1]
    core = jnp.einsum("inr,jns->ijrs", coeff, col_coeff, preferred_element_type=jnp.float32)
    core = core.astype(jnp.bfloat16)
    update = jnp.einsum("jns,ijrs->ijnr", col_left, core, preferred_element_type=jnp.float32)
    return (left, update.astype(jnp.bfloat16))


def solution(mesh):
    in_specs = (P(), P(None, "row", "col"), P("row", "col", None), P())
    out_specs = (P("row", "col", None), P("row", "col", None, None))
    return jax.shard_map(shards, mesh=mesh, in_specs=in_specs, out_specs=out_specs, check_vma=False)
```

profile of v0, /device:TPU:24, one launch (start us, length us, event | category | flops | bytes accessed | tf_op | source)
XLA Modules:
  0.0 1680.3 jit_solution(12171304196142821972)
XLA Ops:
  8.9 7.0 subtract_convert_fusion
  15.9 4.3 iota.299
  20.2 4.8 triangular_solve.302
  25.0 4.8 broadcast.804
  29.8 14.6 conditional.1
  29.8 4.8 broadcast.796
  44.4 4.7 broadcast_select_fusion
  51.7 639.4 %all-reduce.6.cloned.1.call-done = f32[1536,1536]{1,0:T(8,128)} async-done(((f32[1536,1536]{1,0:T(8,128)}), f32[1536,1536]{1,0:T(8,128)}) %all-reduce.6.cloned.1.call-update) | async-done | bytes 9437200 | tf_op jit(solution)/shard_map/psum | solution.py:13
  691.1 8.4 fusion.72
  699.4 35.7 %while.2 = (s32[]{:T(128)}, f32[1536,1536]{1,0:T(8,128)}, s32[12,2]{0,1:T(2,128)S(1)}, f32[12,128,128]{2,1,0:T(8,128)S(1)}, s32[]{:T(128)}) while((s32[]{:T(128)}, f32[1536,1536]{1,0:T(8,128)}, s32[12,2]{0,1:T(2,128)S(1)}, f32[12,128,128]{2,1,0:T(8,128)S(1)}, s32[]{:T(128)}) %tuple.143), condition=%wide.while_cond, body=%wide.while_body.sunk | while | flops 2 | bytes 131181 | solution.py:46
  700.1 2.3 bitcast_dynamic-update-slice_fusion.4
  703.1 2.3 bitcast_dynamic-update-slice_fusion.4
  735.2 117.9 %custom-call.130 = f32[12,128,128]{1,2,0:T(8,128)S(1)} custom-call(f32[12,128,128]{2,1,0:T(8,128)S(1)} %get-tuple-element.41), custom_call_target="InvertDiagBlocksLowerTriangular" | custom-call | tf_op jit(solution)/shard_map/jit(_solve_triangular)/triangular_solve | solution.py:46
  872.9 2.5 fusion.76
  878.2 157.0 %all-reduce.8.cloned.1.call-done = f32[1,512,512]{1,2,0:T(8,128)} async-done(((f32[1,512,512]{1,2,0:T(8,128)}), f32[1,512,512]{1,2,0:T(8,128)}) %all-reduce.8.cloned.1.call-update) | async-done | bytes 1048592 | tf_op jit(solution)/shard_map/psum | solution.py:52
  1035.3 8.6 gather_fusion
  1049.0 11.7 custom-call.131
  1060.8 9.8 custom-call.132
  1071.4 11.7 custom-call.133
  1083.5 10.0 custom-call.134
  1094.4 11.7 custom-call.135
  1106.3 9.8 custom-call.136
  1116.9 11.9 custom-call.137
  1134.3 11.3 while.3
  1145.6 40.1 %custom-call.138 = f32[1,4,128,128]{2,3,1,0:T(8,128)S(1)} custom-call(f32[1,4,128,128]{3,2,1,0:T(8,128)} %bitcast.372), custom_call_target="InvertDiagBlocksLowerTriangular" | custom-call | tf_op jit(solution)/shard_map/vmap(jit(_solve_triangular))/triangular_solve | solution.py:23
  1187.3 4.2 convolution_bitcast_fusion
  1192.3 83.5 %reduce-scatter.2.cloned.1.call-done = f32[1,96,512]{2,1,0:T(8,128)} async-done(((f32[1,1536,512]{2,1,0:T(8,128)}), f32[1,96,512]{2,1,0:T(8,128)}) %reduce-scatter.2.cloned.1.call-update) | async-done | bytes 196624 | tf_op jit(solution)/shard_map/reduce_scatter | solution.py:62
  1277.5 84.0 %all-gather.6.cloned.1.call-done = bf16[1,1536,512]{2,1,0:T(8,128)(2,1)} async-done(((bf16[1,96,512]{2,1,0:T(8,128)(2,1)}), bf16[1,1536,512]{2,1,0:T(8,128)(2,1)}) %all-gather.6.cloned.1.call-update) | async-done | bytes 1572880 | tf_op jit(solution)/shard_map/all_gather | solution.py:66
  1361.5 83.2 %all-gather.8.cloned.1.call-done = bf16[1,1536,512]{2,1,0:T(8,128)(2,1)} async-done(((bf16[1,96,512]{2,1,0:T(8,128)(2,1)}), bf16[1,1536,512]{2,1,0:T(8,128)(2,1)}) %all-gather.8.cloned.1.call-update) | async-done | bytes 1572880 | tf_op jit(solution)/shard_map/all_gather | solution.py:65
  1444.7 4.0 maximum_select_fusion
  1448.7 218.2 %all-reduce.10.cloned.1.call-done = bf16[2,1,1536,512]{3,2,1,0:T(8,128)(2,1)} async-done(((bf16[2,1,1536,512]{3,2,1,0:T(8,128)(2,1)}), bf16[2,1,1536,512]{3,2,1,0:T(8,128)(2,1)}) %all-reduce.10.cloned.1.call-update) | async-done | bytes 3145744 | tf_op jit(solution)/shard_map/psum | solution.py:13
  1666.9 3.8 fusion.73
  (156 shorter events, 83.2 us)
Async XLA Ops:
  8.0 683.1 %all-reduce.6.cloned.1.call-start = ((), (), s32[]{:S(2)}) async-start(), calls=%async_computation.1 | async-start | bytes 18874368 | tf_op jit(solution)/shard_map/psum | solution.py:13
  49.1 0.7 copy-start.2
  49.1 0.7 copy-start.3
  49.1 823.8 %all-gather.4.cloned.1.call-start = ((), (), s32[]{:S(2)}) async-start(), calls=%async_computation.2 | async-start | bytes 1671168 | tf_op jit(solution)/shard_map/all_gather | solution.py:42
  49.7 985.5 %all-reduce.8.cloned.1.call-start = ((), (), s32[]{:S(2)}) async-start(), calls=%async_computation.3 | async-start | bytes 2097152 | tf_op jit(solution)/shard_map/psum | solution.py:52
  872.9 172.3 %copy-start = (f32[1536,96]{0,1:T(8,128)}, f32[1536,96]{0,1:T(8,128)S(1)}, u32[]{:S(2)}) copy-start(f32[1536,96]{0,1:T(8,128)S(1)} %convolution_dynamic-update-slice_fusion.10) | copy-start | bytes 1769476
  877.4 398.4 %reduce-scatter.2.cloned.1.call-start = ((), (), s32[]{:S(2)}) async-start(), calls=%async_computation.5 | async-start | bytes 3342336 | tf_op jit(solution)/shard_map/reduce_scatter | solution.py:62
  1191.5 170.0 %all-gather.6.cloned.1.call-start = ((), (), s32[]{:S(2)}) async-start(), calls=%async_computation.4 | async-start | bytes 1671168 | tf_op jit(solution)/shard_map/all_gather | solution.py:66
  1192.3 252.4 %all-gather.8.cloned.1.call-start = ((), (), s32[]{:S(2)}) async-start(), calls=%async_computation.6 | async-start | bytes 1671168 | tf_op jit(solution)/shard_map/all_gather | solution.py:65
  1277.5 389.4 %all-reduce.10.cloned.1.call-start = ((), (), s32[]{:S(2)}) async-start(), calls=%async_computation.7 | async-start | bytes 6291456 | tf_op jit(solution)/shard_map/psum | solution.py:13
  1444.7 222.2 %copy-start.1 = (bf16[1,1536,512]{2,1,0:T(8,128)(2,1)S(1)}, bf16[1,1536,512]{2,1,0:T(8,128)(2,1)}, u32[]{:S(2)}) copy-start(bf16[1,1536,512]{2,1,0:T(8,128)(2,1)} %all-gather.8.cloned.1.call-done) | copy-start | bytes 4718596
Sparse Core Ops, SparseCore 0:
  49.3 641.7 all-reduce.5
  1448.8 218.0 all-reduce.9
Sparse Core Ops, SparseCore 1:
  51.4 440.1 all-gather.3
  877.5 157.7 all-reduce.7
  1191.6 84.2 reduce-scatter.1
  1278.3 83.2 all-gather.5
  1363.9 80.7 all-gather.7
where the time goes:
time: 1690 us; the launch traced here: 1680 us
  waiting for transfers between devices  1270 us (75%)
  other arithmetic  269 us (16%)
  local copies, waits for them, and re-layouts  78.2 us (5%)
  matrix products  36 us (2%)
  between operations  20.7 us (1%)
    psum x2, waiting for transfers between devices, broadcast(): return lax.psum(jnp.where(mine, value, jnp.zeros_like(value)), axis)  858 us
    psum x1, waiting for transfers between devices, shards(): gram = lax.psum(gram_part, 'col')  157 us
    another operation x3, other arithmetic, shards(): solved = jax.scipy.linalg.solve_triangular(lower, block.T, lower=True).T  126 us
    all_gather x1, waiting for transfers between devices, shards(): left_full = lax.all_gather(left, 'col', axis=1, tiled=True)  84 us
    reduce_scatter x1, waiting for transfers between devices, shards(): lax.psum_scatter(coeff_part, 'col', scatter_dimension=1, tiled=True)  83.5 us
    all_gather x1, waiting for transfers between devices, shards(): coeff = lax.all_gather(coeff_piece, 'col', axis=1, tiled=True)  83.2 us
    another operation x15, other arithmetic, shards(): factor = jnp.linalg.cholesky(shifted)  79.4 us
    another operation x58, local copies, waits for them, and re-layouts  56.4 us
  transfers between devices with their start and end apart: 7, of which 6 were waited for; matrix products, arithmetic and copies ran while one was open for 11% of the time, Pallas kernels for 0%

commit v1 on v0

--- a/solution.py
+++ b/solution.py
@@ -6,6 +6,13 @@
 range_length = 409.6
 nugget = 0.5
 shift_ratio = 0.01
+
+
+def wait_the_slabs(q_in, x0):
+    reply = jnp.concatenate([q_in, x0], axis=0)
+    local_next = lax.all_gather(reply, axis_name="col", axis=1, tiled=True)
+    upper = jnp.split(local_next, [q_in.shape[0]], axis=0)
+    return upper
 
 
 def broadcast(value, axis, root):
@@ -62,8 +69,7 @@
     coeff_piece = lax.psum_scatter(coeff_part, "col", scatter_dimension=1, tiled=True).astype(
         jnp.bfloat16
     )
-    coeff = lax.all_gather(coeff_piece, "col", axis=1, tiled=True)
-    left_full = lax.all_gather(left, "col", axis=1, tiled=True)
+    coeff, left_full = wait_the_slabs(coeff_piece, left)
     root = col_index * col_tiles // row_tiles
     stacked = jnp.stack([left_full, coeff])
     slab = broadcast(stacked, "row", root)

time: 1690 us -> 1610 us (0.953)
  waiting for transfers between devices: 1270 us -> 1190 us
    all_gather x2 -> x1, waiting for transfers between devices: 167 us -> 87.8 us  [wait_the_slabs(): local_next = lax.all_gather(reply, axis_name='col', axis=1, tiled=True)]
    another operation x58 -> x59, local copies, waits for them, and re-layouts: 56.4 us -> 58.6 us
  transfers between devices with their start and end apart: 7 -> 6, of which waited for: 6 -> 5; matrix products, arithmetic and copies ran while one was open for 11% -> 11% of each run, Pallas kernels for 0% -> 0%
where the time goes in v1:
time: 1610 us; the launch traced here: 1600 us
  waiting for transfers between devices  1190 us (74%)
  other arithmetic  267 us (17%)
  local copies, waits for them, and re-layouts  81.5 us (5%)
  matrix products  37.2 us (2%)
  between operations  20.7 us (1%)
    psum x2, waiting for transfers between devices, broadcast(): return lax.psum(jnp.where(mine, value, jnp.zeros_like(value)), axis)  859 us
    psum x1, waiting for transfers between devices, shards(): gram = lax.psum(gram_part, 'col')  157 us
    another operation x3, other arithmetic, shards(): solved = jax.scipy.linalg.solve_triangular(lower, block.T, lower=True).T  126 us
    all_gather x1, waiting for transfers between devices, wait_the_slabs(): local_next = lax.all_gather(reply, axis_name='col', axis=1, tiled=True)  87.8 us
    reduce_scatter x1, waiting for transfers between devices, shards(): lax.psum_scatter(coeff_part, 'col', scatter_dimension=1, tiled=True)  84.3 us
    another operation x15, other arithmetic, shards(): factor = jnp.linalg.cholesky(shifted)  79.4 us
    another operation x58, local copies, waits for them, and re-layouts  56.4 us
    another operation x3, other arithmetic, solve_right(): return jax.scipy.linalg.solve_triangular(factor, sample.T, lower=True).T  40.3 us
  transfers between devices with their start and end apart: 6, of which 5 were waited for; matrix products, arithmetic and copies ran while one was open for 11% of the time, Pallas kernels for 0%

profile of v1, /device:TPU:24, one launch (start us, length us, event | category | flops | bytes accessed | tf_op | source)
XLA Modules:
  0.0 1604.7 jit_solution(934094754466460791)
XLA Ops:
  8.9 7.0 subtract_convert_fusion
  15.9 4.3 iota.299
  20.2 4.8 triangular_solve.302
  25.0 4.8 broadcast.804
  29.8 14.6 conditional.1
  29.8 4.8 broadcast.796
  44.4 4.7 broadcast_select_fusion
  51.7 639.4 %all-reduce.6.cloned.1.call-done = f32[1536,1536]{1,0:T(8,128)} async-done(((f32[1536,1536]{1,0:T(8,128)}), f32[1536,1536]{1,0:T(8,128)}) %all-reduce.6.cloned.1.call-update) | async-done | bytes 9437200 | tf_op jit(solution)/shard_map/psum | solution.py:20
  691.1 8.4 fusion.72
  699.4 35.7 %while.2 = (s32[]{:T(128)}, f32[1536,1536]{1,0:T(8,128)}, s32[12,2]{0,1:T(2,128)S(1)}, f32[12,128,128]{2,1,0:T(8,128)S(1)}, s32[]{:T(128)}) while((s32[]{:T(128)}, f32[1536,1536]{1,0:T(8,128)}, s32[12,2]{0,1:T(2,128)S(1)}, f32[12,128,128]{2,1,0:T(8,128)S(1)}, s32[]{:T(128)}) %tuple.144), condition=%wide.while_cond, body=%wide.while_body.sunk | while | flops 2 | bytes 131181 | solution.py:53
  700.1 2.3 bitcast_dynamic-update-slice_fusion.4
  703.1 2.3 bitcast_dynamic-update-slice_fusion.4
  726.9 2.3 bitcast_dynamic-update-slice_fusion.4
  735.2 117.9 %custom-call.130 = f32[12,128,128]{1,2,0:T(8,128)S(1)} custom-call(f32[12,128,128]{2,1,0:T(8,128)S(1)} %get-tuple-element.41), custom_call_target="InvertDiagBlocksLowerTriangular" | custom-call | tf_op jit(solution)/shard_map/jit(_solve_triangular)/triangular_solve | solution.py:53
  872.9 2.5 fusion.76
  878.2 157.0 %all-reduce.8.cloned.1.call-done = f32[1,512,512]{1,2,0:T(8,128)} async-done(((f32[1,512,512]{1,2,0:T(8,128)}), f32[1,512,512]{1,2,0:T(8,128)}) %all-reduce.8.cloned.1.call-update) | async-done | bytes 1048592 | tf_op jit(solution)/shard_map/psum | solution.py:59
  1035.3 8.6 gather_fusion
  1049.0 11.7 custom-call.131
  1060.8 9.8 custom-call.132
  1071.4 11.7 custom-call.133
  1083.5 10.0 custom-call.134
  1094.4 11.7 custom-call.135
  1106.3 9.8 custom-call.136
  1116.9 11.9 custom-call.137
  1134.3 11.3 while.3
  1145.6 40.1 %custom-call.138 = f32[1,4,128,128]{2,3,1,0:T(8,128)S(1)} custom-call(f32[1,4,128,128]{3,2,1,0:T(8,128)} %bitcast.372), custom_call_target="InvertDiagBlocksLowerTriangular" | custom-call | tf_op jit(solution)/shard_map/vmap(jit(_solve_triangular))/triangular_solve | solution.py:30
  1187.3 4.2 convolution_bitcast_fusion
  1191.6 84.3 %reduce-scatter.2.cloned.1.call-done = f32[1,96,512]{2,1,0:T(8,128)} async-done(((f32[1,1536,512]{2,1,0:T(8,128)}), f32[1,96,512]{2,1,0:T(8,128)}) %reduce-scatter.2.cloned.1.call-update) | async-done | bytes 196624 | tf_op jit(solution)/shard_map/reduce_scatter | solution.py:69
  1277.6 87.8 %all-gather.5.cloned.1.call-done = bf16[2,1536,512]{2,1,0:T(8,128)(2,1)} async-done(((bf16[2,96,512]{2,1,0:T(8,128)(2,1)}), bf16[2,1536,512]{2,1,0:T(8,128)(2,1)}) %all-gather.5.cloned.1.call-update) | async-done | bytes 3145744 | tf_op jit(solution)/shard_map/all_gather | solution.py:13
  1369.7 219.4 %all-reduce.10.cloned.1.call-done = bf16[2,1,1536,512]{3,2,1,0:T(8,128)(2,1)} async-done(((bf16[2,1,1536,512]{3,2,1,0:T(8,128)(2,1)}), bf16[2,1,1536,512]{3,2,1,0:T(8,128)(2,1)}) %all-reduce.10.cloned.1.call-update) | async-done | bytes 3145744 | tf_op jit(solution)/shard_map/psum | solution.py:20
  1589.1 5.0 fusion.73
  1594.1 2.6 copy.29
  (157 shorter events, 82.9 us)
Async XLA Ops:
  8.0 683.1 %all-reduce.6.cloned.1.call-start = ((), (), s32[]{:S(2)}) async-start(), calls=%async_computation.1 | async-start | bytes 18874368 | tf_op jit(solution)/shard_map/psum | solution.py:20
  49.1 0.7 copy-start.3
  49.1 0.7 copy-start.4
  49.1 823.8 %all-gather.3.cloned.1.call-start = ((), (), s32[]{:S(2)}) async-start(), calls=%async_computation.2 | async-start | bytes 1671168 | tf_op jit(solution)/shard_map/all_gather | solution.py:49
  49.7 985.5 %all-reduce.8.cloned.1.call-start = ((), (), s32[]{:S(2)}) async-start(), calls=%async_computation.3 | async-start | bytes 2097152 | tf_op jit(solution)/shard_map/psum | solution.py:59
  872.9 172.3 %copy-start.1 = (f32[1536,96]{0,1:T(8,128)}, f32[1536,96]{0,1:T(8,128)S(1)}, u32[]{:S(2)}) copy-start(f32[1536,96]{0,1:T(8,128)S(1)} %convolution_dynamic-update-slice_fusion.10) | copy-start | bytes 1769476
  877.4 398.4 %reduce-scatter.2.cloned.1.call-start = ((), (), s32[]{:S(2)}) async-start(), calls=%async_computation.4 | async-start | bytes 3342336 | tf_op jit(solution)/shard_map/reduce_scatter | solution.py:69
  1191.5 173.8 %all-gather.5.cloned.1.call-start = ((), (), s32[]{:S(2)}) async-start(), calls=%async_computation.5 | async-start | bytes 3342336 | tf_op jit(solution)/shard_map/all_gather | solution.py:13
  1191.6 402.5 %copy-start.2 = (bf16[1,96,512]{2,1,0:T(8,128)(2,1)}, bf16[1,96,512]{2,1,0:T(8,128)(2,1)S(1)}, u32[]{:S(2)}) copy-start(bf16[1,96,512]{2,1,0:T(8,128)(2,1)S(1)} %fusion.152) | copy-start | bytes 294916
  1277.5 311.5 %all-reduce.10.cloned.1.call-start = ((), (), s32[]{:S(2)}) async-start(), calls=%async_computation.6 | async-start | bytes 6291456 | tf_op jit(solution)/shard_map/psum | solution.py:20
  1365.4 223.7 %copy-start = (bf16[2,1536,512]{2,1,0:T(8,128)(2,1)S(1)}, bf16[2,1536,512]{2,1,0:T(8,128)(2,1)}, u32[]{:S(2)}) copy-start(bf16[2,1536,512]{2,1,0:T(8,128)(2,1)} %all-gather.5.cloned.1.call-done) | copy-start | bytes 9437188
Sparse Core Ops, SparseCore 0:
  49.3 641.7 all-reduce.5
  1369.8 219.2 all-reduce.9
Sparse Core Ops, SparseCore 1:
  51.4 440.1 all-gather.2
  877.5 157.7 all-reduce.7
  1191.6 84.2 reduce-scatter.1
  1278.3 87.0 all-gather.4
